TPU v7x, 256 devices: a whole 4x4x8 slice. The times are simulated.
256 devices in a mesh: view: 16 (over z, y_hi), tok: 16 (over y_lo, x, core).
Axes of the slice: x: 4, y: 4 (y_hi: 2, y_lo: 2; y = y_hi * 2 + y_lo), z: 8, core: 2. Of those that a mesh axis runs over, the one named last changes fastest.
Arguments:
- q1: bfloat16 [16, 512, 1024], P('view', 'tok'), may hold values from -96 to 96
- k1: bfloat16 [16, 512, 1024], P('view', 'tok'), may hold values from -6 to 6
- v1: bfloat16 [16, 512, 1024], P('view', 'tok'), may hold values from -6 to 6
- nbr: int32 [16, 7], P('view'), may hold values from 0 to 15, as said below
- x2: bfloat16 [16, 512, 1024], P('view', 'tok'), may hold values from -6 to 6
- w_view_out: bfloat16 [1024, 1024], replicated, may hold values from -0.1875 to 0.1875
- norm_gain: float32 [1024], replicated, may hold values from 0.5 to 1.5
- w_qkv: bfloat16 [1024, 3072], replicated, may hold values from -0.1875 to 0.1875
- w_out: bfloat16 [1024, 1024], replicated, may hold values from -0.1875 to 0.1875
Outputs:
- view_feats: float32 [16, 512, 1024], P('view', 'tok')
- lrm_out: float32 [16, 512, 1024], P('view', 'tok')
Inputs may be any that keep to these rules, and one draw needn't show every extreme that they name: `nbr`: row v lists 7 distinct view indices, none equal to v.
All inputs are finite; a program needn't handle non-finite values.
Results may differ from a plain program's by a relative error of at most 0.014.
Values may be sent and summed in bfloat16 or wider, within the bound.
A program may use at most 128 MiB of HBM per device.

v0:
```python
import jax
import jax.numpy as jnp
from jax import lax
from jax.sharding import PartitionSpec as P

H1 = 16
HD1 = 64
HD2 = 64
EPSILON = 1e-06
NEGATIVE = -1e30


def absorb(running, queries, key_piece, val_piece, keep_key, factor_scale):
    running_max, row_total, weighted = running
    scores = (
        jnp.einsum("qhd,khd->qhk", queries, key_piece, preferred_element_type=jnp.float32)
        * factor_scale
    )
    scores = jnp.where(keep_key[None, None, :], scores, NEGATIVE)
    new_max = jnp.maximum(running_max, jnp.max(scores, axis=-1))
    weights = jnp.where(keep_key[None, None, :], jnp.exp(scores - new_max[..., None]), 0.0)
    row_total = jnp.sum(weights, axis=-1)
    weighted = jnp.einsum(
        "qhk,khd->qhd", weights.astype(jnp.bfloat16), val_piece, preferred_element_type=jnp.float32
    )
    return (new_max, row_total, weighted)


def per_device(q1, k1, v1, nbr, x2, w_view_out, norm_gain, w_qkv, w_out):
    own_view = lax.axis_index("view")
    wanted = nbr[0]
    queries = lax.all_gather(q1, "tok", axis=1, tiled=True)[0].reshape(-1, H1, HD1)
    query_rows = queries.shape[0]
    start_state = (
        jnp.full((query_rows, H1), NEGATIVE, jnp.float32),
        jnp.zeros((query_rows, H1), jnp.float32),
        jnp.zeros((query_rows, H1, HD1), jnp.float32),
    )
    scale_one = HD1 ** (-0.5)
    key_piece = lax.all_gather(k1, "view", axis=0, tiled=True)
    val_piece = lax.all_gather(v1, "view", axis=0, tiled=True)
    view_ids = jnp.arange(key_piece.shape[0], dtype=jnp.int32)
    keep_view = (view_ids == own_view) | jnp.any(view_ids[:, None] == wanted[None, :], axis=1)
    keep_key = jnp.repeat(keep_view, key_piece.shape[1])
    running_max, row_total, weighted = absorb(
        start_state,
        queries,
        key_piece.reshape(-1, H1, HD1),
        val_piece.reshape(-1, H1, HD1),
        keep_key,
        scale_one,
    )
    tok_devs = lax.axis_size("tok")
    my_rows = query_rows // tok_devs
    row_peak = lax.pmax(running_max, "tok")
    factor = jnp.exp(running_max - row_peak)
    summed, totals = (
        lax.psum_scatter(weighted * factor[..., None], "tok", scatter_dimension=0, tiled=True),
        lax.psum_scatter(row_total * factor, "tok", scatter_dimension=0, tiled=True),
    )
    attn_one = (summed / totals[..., None]).reshape(my_rows, -1)
    features = attn_one * lax.rsqrt(jnp.mean(attn_one * attn_one, axis=-1, keepdims=True) + EPSILON)
    features_half = features.astype(jnp.bfloat16)
    hidden = x2[0].astype(jnp.float32) + jnp.dot(
        features_half, w_view_out, preferred_element_type=jnp.float32
    )
    normed = (
        hidden * lax.rsqrt(jnp.mean(hidden * hidden, axis=-1, keepdims=True) + EPSILON) * norm_gain
    ).astype(jnp.bfloat16)
    projected = (
        jnp.dot(normed, w_qkv, preferred_element_type=jnp.float32)
        .astype(jnp.bfloat16)
        .reshape(my_rows, 3, -1)
    )
    by_head = lax.all_to_all(projected, "tok", split_axis=2, concat_axis=0, tiled=True)
    local_heads = by_head.shape[2] // HD2
    head_queries = by_head[:, 0].reshape(-1, local_heads, HD2)
    view_rows = head_queries.shape[0]
    scale_two = HD2 ** (-0.5)
    second_state = (
        jnp.full((view_rows, local_heads), NEGATIVE, jnp.float32),
        jnp.zeros((view_rows, local_heads), jnp.float32),
        jnp.zeros((view_rows, local_heads, HD2), jnp.float32),
    )
    key_piece = lax.all_gather(by_head[:, 1], "view", axis=0, tiled=True)
    val_piece = lax.all_gather(by_head[:, 2], "view", axis=0, tiled=True)
    keep_key = jnp.ones((key_piece.shape[0],), jnp.bool_)
    second_max, second_total, second_sum = absorb(
        second_state,
        head_queries,
        key_piece.reshape(-1, local_heads, HD2),
        val_piece.reshape(-1, local_heads, HD2),
        keep_key,
        scale_two,
    )
    attn_two = (second_sum / second_total[..., None]).reshape(view_rows, -1).astype(jnp.bfloat16)
    returned = lax.all_to_all(attn_two, "tok", split_axis=0, concat_axis=1, tiled=True)
    wide = returned.astype(jnp.float32)
    unit_rows = (wide * lax.rsqrt(jnp.mean(wide * wide, axis=-1, keepdims=True) + EPSILON)).astype(
        jnp.bfloat16
    )
    result = jnp.dot(unit_rows, w_out, preferred_element_type=jnp.float32)
    return (features[None], result[None])


def solution(mesh):
    return jax.shard_map(
        per_device,
        mesh=mesh,
        in_specs=(
            P("view", "tok", None),
            P("view", "tok", None),
            P("view", "tok", None),
            P("view", None),
            P("view", "tok", None),
            P(),
            P(),
            P(),
            P(),
        ),
        out_specs=(P("view", "tok", None), P("view", "tok", None)),
        check_vma=False,
    )
```

profile of v0, /device:TPU:1, one launch (start us, length us, event | category | flops | bytes accessed | tf_op | source)
XLA Modules:
  0.0 568.1 jit_solution(11776893962329701940)
XLA Ops:
  10.4 78.4 %all-gather.8.cloned.1.call-done = bf16[16,32,1024]{2,1,0:T(8,128)(2,1)} async-done(((bf16[1,32,1024]{2,1,0:T(8,128)(2,1)}), bf16[16,32,1024]{2,1,0:T(8,128)(2,1)}) %all-gather.8.cloned.1.call-update) | async-done | bytes 1048592 | tf_op jit(solution)/shard_map/all_gather | solution.py:40
  88.8 4.1 reshape.120
  92.8 33.8 %all-gather.10.cloned.1.call-done = bf16[1,512,1024]{2,1,0:T(8,128)(2,1)} async-done(((bf16[1,32,1024]{2,1,0:T(8,128)(2,1)}), bf16[1,512,1024]{2,1,0:T(8,128)(2,1)}) %all-gather.10.cloned.1.call-update) | async-done | bytes 1048592 | tf_op jit(solution)/shard_map/all_gather | solution.py:32
  128.1 9.1 %bitcast_reduce_fusion = (f32[512,16]{0,1:T(8,128)S(1)}, f32[16,512,512]{2,1,0:T(8,128)}) fusion(pred[512]{0:T(512)(128)(4,1)S(1)} %broadcast_in_dim.58, bf16[512,16,64]{0,2,1:T(8,128)(2,1)S(1)} %bitcast.104, bf16[512,16,64]{2,1,0:T(8,128)(2,1)} %reshape.120), kind=kOutput, calls=%fused_computation.3 | convolution fusion | flops 549445632 | bytes 18907648 | tf_op jit(solution)/shard_map/qhd,khd->qhk/dot_general | solution.py:16
  137.2 50.7 %pmax.7 = f32[512,16]{0,1:T(8,128)S(1)} all-reduce(f32[512,16]{0,1:T(8,128)S(1)} %broadcast_maximum_fusion), channel_id=1, replica_groups=mesh['view'=16,'tok'=16] {'tok'}, use_global_device_ids=true, to_apply=%region_2.3 | all-reduce | flops 8192 | bytes 65536 | tf_op jit(solution)/shard_map/pmax | solution.py:55
  187.8 8.2 %fusion.5 = f32[512,16]{0,1:T(8,128)S(1)} fusion(f32[16,512,512]{2,1,0:T(8,128)} %get-tuple-element.9, f32[512,16]{0,1:T(8,128)S(1)} %broadcast_maximum_fusion, pred[512]{0:T(512)(128)(4,1)S(1)} %broadcast_in_dim.58), kind=kLoop, calls=%fused_computation.10 | loop fusion | flops 20963328 | bytes 16843264 | tf_op jit(solution)/shard_map/reduce_sum | solution.py:22
  196.9 6.2 %all-gather.12.cloned.1.call-done = bf16[16,32,1024]{2,1,0:T(8,128)(2,1)} async-done(((bf16[1,32,1024]{2,1,0:T(8,128)(2,1)}), bf16[16,32,1024]{2,1,0:T(8,128)(2,1)}) %all-gather.12.cloned.1.call-update) | async-done | bytes 1048592 | tf_op jit(solution)/shard_map/all_gather | solution.py:41
  203.1 4.1 reshape.121
  207.1 11.6 %bitcast_multiply_fusion = f32[512,16,64]{0,2,1:T(8,128)} fusion(f32[16,512,512]{2,1,0:T(8,128)} %get-tuple-element.9, f32[512,16]{0,1:T(8,128)S(1)} %broadcast_maximum_fusion, pred[512]{0:T(512)(128)(4,1)S(1)} %broadcast_in_dim.58, bf16[512,16,64]{2,1,0:T(8,128)(2,1)} %reshape.121, f32[512,16]{0,1:T(8,128)S(1)} %get-tuple-element.5), kind=kOutput, calls=%fused_computation.21 | convolution fusion | flops 558366720 | bytes 19988992 | tf_op jit(solution)/shard_map/qhk,khd->qhd/dot_general | solution.py:23
  218.8 4.8 copy.60
  223.9 42.9 %reduce-scatter.7.cloned.1.call-done = f32[32,16]{1,0:T(8,128)} async-done(((f32[512,16]{1,0:T(8,128)}), f32[32,16]{1,0:T(8,128)}) %reduce-scatter.7.cloned.1.call-update) | async-done | bytes 2064 | tf_op jit(solution)/shard_map/reduce_scatter | solution.py:59
  266.7 70.7 %reduce-scatter.5.cloned.1.call-done = f32[32,16,64]{2,1,0:T(8,128)} async-done(((f32[512,16,64]{2,1,0:T(8,128)}), f32[32,16,64]{2,1,0:T(8,128)}) %reduce-scatter.5.cloned.1.call-update) | async-done | bytes 131088 | tf_op jit(solution)/shard_map/reduce_scatter | solution.py:58
  339.7 4.0 convolution_convert_fusion
  344.7 1.8 copy.62
  347.9 14.7 %all_to_all.28 = bf16[16,2,3072]{2,1,0:T(2,128)(2,1)} all-to-all(bf16[16,2,3072]{2,1,0:T(2,128)(2,1)} %reshape.133), channel_id=1, replica_groups=mesh['view'=16,'tok'=16] {'tok'}, dimensions={0} | all-to-all | bytes 393216 | tf_op jit(solution)/shard_map/all_to_all | solution.py:75
  365.4 1.7 fusion.55
  368.0 79.9 %all-gather.16.cloned.1.call-done = bf16[8192,1,64]{2,0,1:T(8,128)(2,1)} async-done(((bf16[512,1,64]{2,0,1:T(8,128)(2,1)}), bf16[8192,1,64]{2,0,1:T(8,128)(2,1)}) %all-gather.16.cloned.1.call-update) | async-done | bytes 1048592 | tf_op jit(solution)/shard_map/all_gather | solution.py:85
  447.9 9.6 %multiply_reduce_fusion = (f32[512]{0:T(512)S(1)}, f32[8192,512]{1,0:T(8,128)}) fusion(bf16[512,3,64]{2,0,1:T(8,128)(2,1)} %bitcast.108, bf16[8192,1,64]{2,0,1:T(8,128)(2,1)} %all-gather.16.cloned.1.call-done), kind=kOutput, calls=%fused_computation.7 | convolution fusion | flops 545259008 | bytes 19007488 | tf_op jit(solution)/shard_map/qhd,khd->qhk/dot_general | solution.py:16
  457.6 8.6 %fusion.3 = f32[512]{0:T(512)S(1)} fusion(f32[8192,512]{1,0:T(8,128)} %get-tuple-element.13, f32[512]{0:T(512)S(1)} %broadcast_maximum_fusion.1), kind=kLoop, calls=%fused_computation.8 | loop fusion | flops 12582400 | bytes 16781312 | tf_op jit(solution)/shard_map/reduce_sum | solution.py:22
  466.2 67.0 %all-gather.14.cloned.1.call-done = bf16[8192,1,64]{2,0,1:T(8,128)(2,1)} async-done(((bf16[512,1,64]{2,0,1:T(8,128)(2,1)}), bf16[8192,1,64]{2,0,1:T(8,128)(2,1)}) %all-gather.14.cloned.1.call-update) | async-done | bytes 1048592 | tf_op jit(solution)/shard_map/all_gather | solution.py:86
  533.2 9.3 %fusion.39 = bf16[512,1,64]{0,2,1:T(8,128)(2,1)S(1)} fusion(f32[8192,512]{1,0:T(8,128)} %get-tuple-element.13, f32[512]{0:T(512)S(1)} %broadcast_maximum_fusion.1, bf16[8192,1,64]{2,0,1:T(8,128)(2,1)} %all-gather.14.cloned.1.call-done, f32[512]{0:T(512)S(1)} %fusion.3), kind=kOutput, calls=%fused_computation.30 | convolution fusion | flops 549519360 | bytes 17895424 | tf_op jit(solution)/shard_map/qhk,khd->qhd/dot_general | solution.py:23
  543.4 8.6 %all-to-all-start.1 = ((bf16[16,2,1024]{2,1,0:T(2,128)(2,1)}), bf16[16,2,1024]{2,1,0:T(2,128)(2,1)S(1)}, u32[]{:S(2)}, u32[]{:S(2)}) async-start(bf16[16,2,1024]{2,1,0:T(2,128)(2,1)} %reshape.135), calls=%async_computation.2 | async-start | bytes 131072 | tf_op jit(solution)/shard_map/all_to_all | solution.py:97
  552.8 5.1 all-to-all-done.1
  558.5 2.8 convolution_bitcast_fusion
  (48 shorter events, 16.3 us)
Async XLA Ops:
  7.2 331.9 %copy-start = (bf16[1024,1024]{1,0:T(8,128)(2,1)S(1)}, bf16[1024,1024]{1,0:T(8,128)(2,1)}, u32[]{:S(2)}) copy-start(bf16[1024,1024]{1,0:T(8,128)(2,1)} %param.14) | copy-start | bytes 6291460
  7.2 81.6 %all-gather.8.cloned.1.call-start = ((), (), s32[]{:S(2)}) async-start(), calls=%async_computation.4 | async-start | bytes 1114112 | tf_op jit(solution)/shard_map/all_gather | solution.py:40
  7.9 118.7 %all-gather.10.cloned.1.call-start = ((), (), s32[]{:S(2)}) async-start(), calls=%async_computation.5 | async-start | bytes 1114112 | tf_op jit(solution)/shard_map/all_gather | solution.py:32
  8.7 194.4 %all-gather.12.cloned.1.call-start = ((), (), s32[]{:S(2)}) async-start(), calls=%async_computation.6 | async-start | bytes 1114112 | tf_op jit(solution)/shard_map/all_gather | solution.py:41
  9.4 257.3 %reduce-scatter.7.cloned.1.call-start = ((), (), s32[]{:S(2)}) async-start(), calls=%async_computation.10 | async-start | bytes 278528 | tf_op jit(solution)/shard_map/reduce_scatter | solution.py:59
  196.9 140.5 %reduce-scatter.5.cloned.1.call-start = ((), (), s32[]{:S(2)}) async-start(), calls=%async_computation.7 | async-start | bytes 4456448 | tf_op jit(solution)/shard_map/reduce_scatter | solution.py:58
  207.1 131.9 %copy-start.1 = (bf16[1,32,1024]{2,1,0:T(8,128)(2,1)S(1)}, bf16[1,32,1024]{2,1,0:T(8,128)(2,1)}, u32[]{:S(2)}) copy-start(bf16[1,32,1024]{2,1,0:T(8,128)(2,1)} %param.13) | copy-start | bytes 196612
  207.1 132.6 %copy-start.2 = (f32[1024]{0:T(1024)S(1)}, f32[1024]{0:T(1024)}, u32[]{:S(2)}) copy-start(f32[1024]{0:T(1024)} %param.15) | copy-start | bytes 12292
  223.6 224.3 %all-gather.16.cloned.1.call-start = ((), (), s32[]{:S(2)}) async-start(), calls=%async_computation.9 | async-start | bytes 2228224 | tf_op jit(solution)/shard_map/all_gather | solution.py:85
  367.1 166.1 %all-gather.14.cloned.1.call-start = ((), (), s32[]{:S(2)}) async-start(), calls=%async_computation.8 | async-start | bytes 2228224 | tf_op jit(solution)/shard_map/all_gather | solution.py:86
  543.4 14.4 %all-to-all-start.1 = ((bf16[16,2,1024]{2,1,0:T(2,128)(2,1)}), bf16[16,2,1024]{2,1,0:T(2,128)(2,1)S(1)}, u32[]{:S(2)}, u32[]{:S(2)}) async-start(bf16[16,2,1024]{2,1,0:T(2,128)(2,1)} %reshape.135), calls=%async_computation.2 | async-start | bytes 131072 | tf_op jit(solution)/shard_map/all_to_all | solution.py:97
Sparse Core Ops, SparseCore 0:
  10.6 78.1 all-gather.7
  90.6 35.9 all-gather.9
  129.2 73.8 all-gather.11
  205.4 61.2 reduce-scatter.6
  269.1 68.2 reduce-scatter.4
  367.3 80.6 all-gather.15
  451.1 82.0 all-gather.13
where the time goes:
time: 569 us; the launch traced here: 568 us
  waiting for transfers between devices  387 us (68%)
  blocking collectives  65.4 us (11%)
  matrix products  47.1 us (8%)
  local copies, waits for them, and re-layouts  25.7 us (5%)
  other arithmetic  20 us (4%)
  between operations  14.3 us (3%)
  starting transfers between devices  9.04 us (2%)
    all_gather x1, waiting for transfers between devices, per_device(): key_piece = lax.all_gather(by_head[:, 1], 'view', axis=0, tiled=True)  79.9 us
    all_gather x1, waiting for transfers between devices, per_device(): key_piece = lax.all_gather(k1, 'view', axis=0, tiled=True)  78.4 us
    reduce_scatter x1, waiting for transfers between devices, per_device(): lax.psum_scatter(weighted * factor[..., None], 'tok', scatter_dimension=0...  70.7 us
    all_gather x1, waiting for transfers between devices, per_device(): val_piece = lax.all_gather(by_head[:, 2], 'view', axis=0, tiled=True)  67 us
    pmax x1, blocking collectives, per_device(): row_peak = lax.pmax(running_max, 'tok')  50.7 us
    reduce_scatter x1, waiting for transfers between devices, per_device(): lax.psum_scatter(row_total * factor, 'tok', scatter_dimension=0, tiled=True)  42.9 us
    all_gather x1, waiting for transfers between devices, per_device(): lax.all_gather(q1, 'tok', axis=1, tiled=True)[0].reshape(-1, H1, HD1)  33.8 us
    dot_general x2, matrix products, absorb(): jnp.einsum('qhk,khd->qhd', weights.astype(jnp.bfloat16), val_piece, prefe...  21 us
  transfers between devices with their start and end apart: 8, of which 8 were waited for; matrix products, arithmetic and copies ran while one was open for 11% of the time, Pallas kernels for 0%

commit v1 on v0

--- a/solution.py
+++ b/solution.py
@@ -37,8 +37,11 @@
         jnp.zeros((query_rows, H1, HD1), jnp.float32),
     )
     scale_one = HD1 ** (-0.5)
-    key_piece = lax.all_gather(k1, "view", axis=0, tiled=True)
-    val_piece = lax.all_gather(v1, "view", axis=0, tiled=True)
+    key_piece, val_piece = jnp.split(
+        lax.all_gather(jnp.concatenate([k1, v1], axis=1), "view", axis=0, tiled=True),
+        [k1.shape[1]],
+        axis=1,
+    )
     view_ids = jnp.arange(key_piece.shape[0], dtype=jnp.int32)
     keep_view = (view_ids == own_view) | jnp.any(view_ids[:, None] == wanted[None, :], axis=1)
     keep_key = jnp.repeat(keep_view, key_piece.shape[1])

time: 569 us -> 574 us (level)
    all_gather x2 -> x1, waiting for transfers between devices: 84.5 us -> 83 us  [per_device(): lax.all_gather(jnp.concatenate([k1, v1], axis=1), 'view', axis=0, tiled=T...]
  transfers between devices with their start and end apart: 8 -> 7, of which waited for: 8 -> 7; matrix products, arithmetic and copies ran while one was open for 11% -> 7% of each run, Pallas kernels for 0% -> 0%
where the time goes in v1:
time: 574 us
  waiting for transfers between devices  387 us (67%)
  blocking collectives  67.4 us (12%)
  matrix products  47.1 us (8%)
  local copies, waits for them, and re-layouts  27.2 us (5%)
  other arithmetic  21.5 us (4%)
  between operations  14.2 us (2%)
  starting transfers between devices  9.01 us (2%)
    all_gather x1, waiting for transfers between devices, per_device(): lax.all_gather(jnp.concatenate([k1, v1], axis=1), 'view', axis=0, tiled=T...  83 us
    all_gather x1, waiting for transfers between devices, per_device(): key_piece = lax.all_gather(by_head[:, 1], 'view', axis=0, tiled=True)  80.1 us
    reduce_scatter x1, waiting for transfers between devices, per_device(): lax.psum_scatter(weighted * factor[..., None], 'tok', scatter_dimension=0...  70.6 us
    all_gather x1, waiting for transfers between devices, per_device(): val_piece = lax.all_gather(by_head[:, 2], 'view', axis=0, tiled=True)  66.9 us
    pmax x1, blocking collectives, per_device(): row_peak = lax.pmax(running_max, 'tok')  52.7 us
    reduce_scatter x1, waiting for transfers between devices, per_device(): lax.psum_scatter(row_total * factor, 'tok', scatter_dimension=0, tiled=True)  42 us
    all_gather x1, waiting for transfers between devices, per_device(): lax.all_gather(q1, 'tok', axis=1, tiled=True)[0].reshape(-1, H1, HD1)  38.3 us
    dot_general x2, matrix products, absorb(): jnp.einsum('qhk,khd->qhd', weights.astype(jnp.bfloat16), val_piece, prefe...  21 us
  transfers between devices with their start and end apart: 7, of which 7 were waited for; matrix products, arithmetic and copies ran while one was open for 7% of the time, Pallas kernels for 0%

profile of v1, /device:TPU:1, one launch (start us, length us, event | category | flops | bytes accessed | tf_op | source)
XLA Modules:
  0.0 573.7 jit_solution(1088139318868740372)
XLA Ops:
  10.5 38.3 %all-gather.9.cloned.1.call-done = bf16[1,512,1024]{2,1,0:T(8,128)(2,1)} async-done(((bf16[1,32,1024]{2,1,0:T(8,128)(2,1)}), bf16[1,512,1024]{2,1,0:T(8,128)(2,1)}) %all-gather.9.cloned.1.call-update) | async-done | bytes 1048592 | tf_op jit(solution)/shard_map/all_gather | solution.py:32
  50.3 83.0 %all-gather.7.cloned.1.call-done = bf16[16,64,1024]{2,1,0:T(8,128)(2,1)} async-done(((bf16[1,64,1024]{2,1,0:T(8,128)(2,1)}), bf16[16,64,1024]{2,1,0:T(8,128)(2,1)}) %all-gather.7.cloned.1.call-update) | async-done | bytes 2097168 | tf_op jit(solution)/shard_map/all_gather | solution.py:41
  133.3 3.2 fusion.55
  136.5 4.1 reshape.121
  140.5 9.1 %bitcast_reduce_fusion = (f32[512,16]{0,1:T(8,128)S(1)}, f32[16,512,512]{2,1,0:T(8,128)}) fusion(pred[512]{0:T(512)(128)(4,1)S(1)} %broadcast_in_dim.58, bf16[512,16,64]{0,2,1:T(8,128)(2,1)S(1)} %bitcast.104, bf16[512,16,64]{2,1,0:T(8,128)(2,1)} %reshape.121), kind=kOutput, calls=%fused_computation.3 | convolution fusion | flops 549445632 | bytes 18907648 | tf_op jit(solution)/shard_map/qhd,khd->qhk/dot_general | solution.py:16
  149.6 52.7 %pmax.7 = f32[512,16]{0,1:T(8,128)S(1)} all-reduce(f32[512,16]{0,1:T(8,128)S(1)} %broadcast_maximum_fusion), channel_id=1, replica_groups=mesh['view'=16,'tok'=16] {'tok'}, use_global_device_ids=true, to_apply=%region_2.3 | all-reduce | flops 8192 | bytes 65536 | tf_op jit(solution)/shard_map/pmax | solution.py:58
  202.3 8.2 %fusion.5 = f32[512,16]{0,1:T(8,128)S(1)} fusion(f32[16,512,512]{2,1,0:T(8,128)} %get-tuple-element.11, f32[512,16]{0,1:T(8,128)S(1)} %broadcast_maximum_fusion, pred[512]{0:T(512)(128)(4,1)S(1)} %broadcast_in_dim.58), kind=kLoop, calls=%fused_computation.10 | loop fusion | flops 20963328 | bytes 16843264 | tf_op jit(solution)/shard_map/reduce_sum | solution.py:22
  210.6 2.4 reshape.120
  213.9 11.6 %bitcast_multiply_fusion = f32[512,16,64]{0,2,1:T(8,128)} fusion(f32[16,512,512]{2,1,0:T(8,128)} %get-tuple-element.11, f32[512,16]{0,1:T(8,128)S(1)} %broadcast_maximum_fusion, pred[512]{0:T(512)(128)(4,1)S(1)} %broadcast_in_dim.58, bf16[512,16,64]{2,1,0:T(8,128)(2,1)} %reshape.120, f32[512,16]{0,1:T(8,128)S(1)} %get-tuple-element.5), kind=kOutput, calls=%fused_computation.21 | convolution fusion | flops 558366720 | bytes 19988992 | tf_op jit(solution)/shard_map/qhk,khd->qhd/dot_general | solution.py:23
  225.5 4.9 copy.60
  230.6 42.0 %reduce-scatter.7.cloned.1.call-done = f32[32,16]{1,0:T(8,128)} async-done(((f32[512,16]{1,0:T(8,128)}), f32[32,16]{1,0:T(8,128)}) %reduce-scatter.7.cloned.1.call-update) | async-done | bytes 2064 | tf_op jit(solution)/shard_map/reduce_scatter | solution.py:62
  272.6 70.6 %reduce-scatter.5.cloned.1.call-done = f32[32,16,64]{2,1,0:T(8,128)} async-done(((f32[512,16,64]{2,1,0:T(8,128)}), f32[32,16,64]{2,1,0:T(8,128)}) %reduce-scatter.5.cloned.1.call-update) | async-done | bytes 131088 | tf_op jit(solution)/shard_map/reduce_scatter | solution.py:61
  345.5 4.0 convolution_convert_fusion
  350.5 1.8 copy.62
  353.6 14.7 %all_to_all.28 = bf16[16,2,3072]{2,1,0:T(2,128)(2,1)} all-to-all(bf16[16,2,3072]{2,1,0:T(2,128)(2,1)} %reshape.133), channel_id=1, replica_groups=mesh['view'=16,'tok'=16] {'tok'}, dimensions={0} | all-to-all | bytes 393216 | tf_op jit(solution)/shard_map/all_to_all | solution.py:78
  371.2 1.7 fusion.56
  373.6 80.1 %all-gather.13.cloned.1.call-done = bf16[8192,1,64]{2,0,1:T(8,128)(2,1)} async-done(((bf16[512,1,64]{2,0,1:T(8,128)(2,1)}), bf16[8192,1,64]{2,0,1:T(8,128)(2,1)}) %all-gather.13.cloned.1.call-update) | async-done | bytes 1048592 | tf_op jit(solution)/shard_map/all_gather | solution.py:88
  453.7 9.6 %multiply_reduce_fusion = (f32[512]{0:T(512)S(1)}, f32[8192,512]{1,0:T(8,128)}) fusion(bf16[512,3,64]{2,0,1:T(8,128)(2,1)} %bitcast.108, bf16[8192,1,64]{2,0,1:T(8,128)(2,1)} %all-gather.13.cloned.1.call-done), kind=kOutput, calls=%fused_computation.7 | convolution fusion | flops 545259008 | bytes 19007488 | tf_op jit(solution)/shard_map/qhd,khd->qhk/dot_general | solution.py:16
  463.3 8.6 %fusion.3 = f32[512]{0:T(512)S(1)} fusion(f32[8192,512]{1,0:T(8,128)} %get-tuple-element.15, f32[512]{0:T(512)S(1)} %broadcast_maximum_fusion.1), kind=kLoop, calls=%fused_computation.8 | loop fusion | flops 12582400 | bytes 16781312 | tf_op jit(solution)/shard_map/reduce_sum | solution.py:22
  471.9 66.9 %all-gather.11.cloned.1.call-done = bf16[8192,1,64]{2,0,1:T(8,128)(2,1)} async-done(((bf16[512,1,64]{2,0,1:T(8,128)(2,1)}), bf16[8192,1,64]{2,0,1:T(8,128)(2,1)}) %all-gather.11.cloned.1.call-update) | async-done | bytes 1048592 | tf_op jit(solution)/shard_map/all_gather | solution.py:89
  538.8 9.3 %fusion.39 = bf16[512,1,64]{0,2,1:T(8,128)(2,1)S(1)} fusion(f32[8192,512]{1,0:T(8,128)} %get-tuple-element.15, f32[512]{0:T(512)S(1)} %broadcast_maximum_fusion.1, bf16[8192,1,64]{2,0,1:T(8,128)(2,1)} %all-gather.11.cloned.1.call-done, f32[512]{0:T(512)S(1)} %fusion.3), kind=kOutput, calls=%fused_computation.30 | convolution fusion | flops 549519360 | bytes 17895424 | tf_op jit(solution)/shard_map/qhk,khd->qhd/dot_general | solution.py:23
  549.0 8.6 %all-to-all-start.1 = ((bf16[16,2,1024]{2,1,0:T(2,128)(2,1)}), bf16[16,2,1024]{2,1,0:T(2,128)(2,1)S(1)}, u32[]{:S(2)}, u32[]{:S(2)}) async-start(bf16[16,2,1024]{2,1,0:T(2,128)(2,1)} %reshape.135), calls=%async_computation.2 | async-start | bytes 131072 | tf_op jit(solution)/shard_map/all_to_all | solution.py:100
  558.4 5.1 all-to-all-done.1
  564.1 2.8 convolution_bitcast_fusion
  (49 shorter events, 16.3 us)
Async XLA Ops:
  7.2 337.7 %copy-start = (bf16[1024,1024]{1,0:T(8,128)(2,1)S(1)}, bf16[1024,1024]{1,0:T(8,128)(2,1)}, u32[]{:S(2)}) copy-start(bf16[1024,1024]{1,0:T(8,128)(2,1)} %param.14) | copy-start | bytes 6291460
  7.2 41.6 %all-gather.9.cloned.1.call-start = ((), (), s32[]{:S(2)}) async-start(), calls=%async_computation.5 | async-start | bytes 1114112 | tf_op jit(solution)/shard_map/all_gather | solution.py:32
  7.9 125.3 %all-gather.7.cloned.1.call-start = ((), (), s32[]{:S(2)}) async-start(), calls=%async_computation.4 | async-start | bytes 2228224 | tf_op jit(solution)/shard_map/all_gather | solution.py:41
  9.5 263.1 %reduce-scatter.7.cloned.1.call-start = ((), (), s32[]{:S(2)}) async-start(), calls=%async_computation.9 | async-start | bytes 278528 | tf_op jit(solution)/shard_map/reduce_scatter | solution.py:62
  202.3 8.2 %copy-start.1 = (bf16[16,32,1024]{2,1,0:T(8,128)(2,1)S(1)}, bf16[16,32,1024]{2,1,0:T(8,128)(2,1)}, u32[]{:S(2)}) copy-start(bf16[16,32,1024]{2,1,0:T(8,128)(2,1)} %get-tuple-element.6) | copy-start | bytes 3145732
  213.8 129.4 %reduce-scatter.5.cloned.1.call-start = ((), (), s32[]{:S(2)}) async-start(), calls=%async_computation.6 | async-start | bytes 4456448 | tf_op jit(solution)/shard_map/reduce_scatter | solution.py:61
  225.5 119.3 %copy-start.2 = (bf16[1,32,1024]{2,1,0:T(8,128)(2,1)S(1)}, bf16[1,32,1024]{2,1,0:T(8,128)(2,1)}, u32[]{:S(2)}) copy-start(bf16[1,32,1024]{2,1,0:T(8,128)(2,1)} %param.13) | copy-start | bytes 196612
  225.5 120.0 %copy-start.3 = (f32[1024]{0:T(1024)S(1)}, f32[1024]{0:T(1024)}, u32[]{:S(2)}) copy-start(f32[1024]{0:T(1024)} %param.15) | copy-start | bytes 12292
  230.4 223.3 %all-gather.13.cloned.1.call-start = ((), (), s32[]{:S(2)}) async-start(), calls=%async_computation.8 | async-start | bytes 2228224 | tf_op jit(solution)/shard_map/all_gather | solution.py:88
  372.9 165.9 %all-gather.11.cloned.1.call-start = ((), (), s32[]{:S(2)}) async-start(), calls=%async_computation.7 | async-start | bytes 2228224 | tf_op jit(solution)/shard_map/all_gather | solution.py:89
  549.0 14.4 %all-to-all-start.1 = ((bf16[16,2,1024]{2,1,0:T(2,128)(2,1)}), bf16[16,2,1024]{2,1,0:T(2,128)(2,1)S(1)}, u32[]{:S(2)}, u32[]{:S(2)}) async-start(bf16[16,2,1024]{2,1,0:T(2,128)(2,1)} %reshape.135), calls=%async_computation.2 | async-start | bytes 131072 | tf_op jit(solution)/shard_map/all_to_all | solution.py:100
Sparse Core Ops, SparseCore 0:
  9.8 38.9 all-gather.8
  52.0 81.2 all-gather.6
  213.9 58.6 reduce-scatter.6
  275.0 68.1 reduce-scatter.4
  373.0 80.6 all-gather.12
  456.7 82.0 all-gather.10
